TPU v7x, 32 devices: a whole 2x2x4 slice. The times are simulated.
32 devices in a mesh: dp: 4 (over x, core), ctx: 4 (over z), tensor: 2 (over y).
Axes of the slice: x: 2, y: 2, z: 4, core: 2. Of those that a mesh axis runs over, the one named last changes fastest.
Arguments:
- block_input: bfloat16 [12288, 2048], P(('dp', 'ctx'), 'tensor'), may hold values from -6 to 6
- cotangent: bfloat16 [12288, 2048], P(('dp', 'ctx'), 'tensor'), may hold values from -6 to 6
- deal_order: int32 [4, 4], P('dp'), may hold values from 0 to 3, as said below
- seq_lengths: int32 [12], P('dp'), may hold values from 96 to 2880, as said below
- seq_adapter: int32 [12], P('dp'), may hold values from 0 to 7
- mixer_gain: bfloat16 [2048], replicated, may hold values from 0.099609375 to 1.8984375
- ffn_gain: bfloat16 [2048], replicated, may hold values from 0.099609375 to 1.8984375
- conv_taps: bfloat16 [3, 2048], P(None, 'tensor'), may hold values from -3.5 to 3.5
- in_weight: bfloat16 [3, 2048, 2048], P(None, 'dp', 'tensor'), may hold values from -0.125 to 0.125
- out_weight: bfloat16 [2048, 2048], P('tensor', 'dp'), may hold values from -0.125 to 0.125
- gateup_weight: bfloat16 [2, 2048, 5632], P(None, 'dp', 'tensor'), may hold values from -0.125 to 0.125
- down_weight: bfloat16 [5632, 2048], P('tensor', 'dp'), may hold values from -0.078125 to 0.078125
- input_adapter_shrink: bfloat16 [2048, 128], replicated, may hold values from -0.125 to 0.125
- in_expand: bfloat16 [3, 128, 2048], P(None, None, 'tensor'), may hold values from -1.5 to 1.5
- out_shrink: bfloat16 [2048, 128], P('tensor'), may hold values from -0.125 to 0.125
- output_adapter_expand: bfloat16 [128, 2048], replicated, may hold values from -1.5 to 1.5
- ffn_shrink: bfloat16 [2048, 256], replicated, may hold values from -0.125 to 0.125
- ffn_expand: bfloat16 [2, 128, 5632], P(None, None, 'tensor'), may hold values from -1.5 to 1.5
- down_shrink: bfloat16 [5632, 128], P('tensor'), may hold values from -0.078125 to 0.078125
- down_adapter_expand: bfloat16 [128, 2048], replicated, may hold values from -1.5 to 1.5
Outputs:
- block_output: bfloat16 [12288, 2048], P(('dp', 'ctx'), 'tensor')
- input_grad: float32 [12288, 2048], P(('dp', 'ctx'), 'tensor')
- in_shrink_grad: float32 [2048, 128], replicated
- input_expand_gradient: float32 [3, 128, 2048], P(None, None, 'tensor')
- out_shrink_grad: float32 [2048, 128], P('tensor')
- output_expand_gradient: float32 [128, 2048], replicated
- ffn_shrink_grad: float32 [2048, 256], replicated
- feedforward_expand_gradient: float32 [2, 128, 5632], P(None, None, 'tensor')
- down_shrink_grad: float32 [5632, 128], P('tensor')
- down_adapter_expand_gradient: float32 [128, 2048], replicated
Inputs may be any that keep to these rules, and one draw needn't show every extreme that they name: `deal_order`: each row is a permutation of the 4 shard numbers. `seq_lengths`: each data group's 3 entries sum to 3072; all but one of them lie between 96 and 192.
All inputs are finite; a program needn't handle non-finite values.
Results may differ from a plain program's by a relative error of at most 0.013.
Values may be sent and summed in bfloat16 or wider, within the bound.
No kernel may reach another device: no remote copies, remote signals or barrier semaphores. Data moves between devices by JAX's collectives and lax.ppermute only.
A program may use at most 256 MiB of HBM per device.

v0:
```python
import jax
import jax.numpy as jnp
from jax import lax
from jax.sharding import PartitionSpec as P

RANK = 16
norm_eps = 1e-05
adapter_scale = 0.5


def shifted(block, axis, distance):
    devices = range(lax.axis_size(axis))
    route = [(i - distance, i) for i in devices if i - distance in devices]
    return lax.ppermute(block, axis, route)


def rms_scale(values):
    return lax.rsqrt(jnp.mean(values * values, axis=-1, keepdims=True) + norm_eps)


def norm_back(values, scale, gain, grad_out):
    unit = values * scale
    grad_unit = grad_out * gain
    return scale * (grad_unit - unit * jnp.mean(grad_unit * unit, axis=-1, keepdims=True))


def product_simple(left, right):
    return jnp.dot(left, right, preferred_element_type=jnp.float32)


def product_backward(left, right):
    return lax.dot_general(
        left, right, (((1,), (1,)), ((), ())), preferred_element_type=jnp.float32
    )


def product_leading(left, right):
    return lax.dot_general(
        left, right, (((0,), (0,)), ((), ())), preferred_element_type=jnp.float32
    )


def segment_of(positions, seq_ends):
    return jnp.sum((positions[:, None] >= seq_ends[None, :]).astype(jnp.int32), axis=1)


def fetch_mixer(in_weight, out_weight):
    return (
        lax.all_gather(in_weight, "dp", axis=1, tiled=True),
        lax.all_gather(out_weight, "dp", axis=1, tiled=True),
    )


def fetch_ffn(gateup_weight, down_weight):
    return (
        lax.all_gather(gateup_weight, "dp", axis=1, tiled=True),
        lax.all_gather(down_weight, "dp", axis=1, tiled=True),
    )


def body(
    block_input,
    cotangent,
    deal_order,
    seq_lengths,
    seq_adapter,
    mixer_gain,
    ffn_gain,
    conv_taps,
    in_weight,
    out_weight,
    gateup_weight,
    down_weight,
    input_adapter_shrink,
    in_expand,
    out_shrink,
    output_adapter_expand,
    ffn_shrink,
    ffn_expand,
    down_shrink,
    down_adapter_expand,
):
    tok_count = block_input.shape[0]
    half_width = block_input.shape[1]
    rank_cols = input_adapter_shrink.shape[1]
    part_index = lax.axis_index("tensor")
    group_total = lax.axis_size("dp")
    block_rows = tok_count // group_total
    deal_row = deal_order[0]
    slot_all = jnp.arange(group_total, dtype=jnp.int32)
    inverse_row = jnp.sum(
        jnp.where(deal_row[:, None] == slot_all[None, :], slot_all[:, None], 0), axis=0
    )
    dealt_in, dealt_cot = (
        lax.all_to_all(
            block_input.reshape(group_total, block_rows, half_width),
            "dp",
            split_axis=0,
            concat_axis=0,
            tiled=True,
        ),
        lax.all_to_all(
            cotangent.reshape(group_total, block_rows, half_width),
            "dp",
            split_axis=0,
            concat_axis=0,
            tiled=True,
        ),
    )
    packed_in = jnp.take(dealt_in, deal_row, axis=0).reshape(tok_count, half_width)
    packed_cot = jnp.take(dealt_cot, deal_row, axis=0).reshape(tok_count, half_width)
    seq_ends = jnp.cumsum(seq_lengths)[:-1]
    positions = lax.axis_index("ctx") * tok_count + jnp.arange(tok_count, dtype=jnp.int32)
    segment = segment_of(positions, seq_ends)
    slot_ids = jnp.arange(seq_lengths.shape[0], dtype=jnp.int32)
    token_adapter_index = jnp.sum(
        jnp.where(segment[:, None] == slot_ids[None, :], seq_adapter[None, :], 0), axis=1
    )
    column_group_index = jnp.arange(rank_cols, dtype=jnp.int32) // RANK
    adapter_mask = (column_group_index[None, :] == token_adapter_index[:, None]).astype(jnp.float32)
    adapter_half_float = adapter_mask.astype(jnp.bfloat16)
    adapter_mask_pair = jnp.concatenate([adapter_mask, adapter_mask], axis=1)
    pair_bf = adapter_mask_pair.astype(jnp.bfloat16)
    matching_first = ((positions >= 1) & (segment_of(positions - 1, seq_ends) == segment)).astype(
        jnp.float32
    )[:, None]
    matching_second = ((positions >= 2) & (segment_of(positions - 2, seq_ends) == segment)).astype(
        jnp.float32
    )[:, None]
    ahead_one = (segment_of(positions + 1, seq_ends) == segment).astype(jnp.float32)[:, None]
    ahead_two = (segment_of(positions + 2, seq_ends) == segment).astype(jnp.float32)[:, None]
    row_pair = (
        lax.all_gather(packed_in, "tensor", axis=1, tiled=True),
        lax.all_gather(packed_cot, "tensor", axis=1, tiled=True),
    )
    input_complete = row_pair[0].astype(jnp.float32)
    cotangent_half_float = row_pair[1]
    cot_full = cotangent_half_float.astype(jnp.float32)
    mixer_f = mixer_gain.astype(jnp.float32)
    ffn_f = ffn_gain.astype(jnp.float32)
    conv_w = conv_taps.astype(jnp.float32)
    in_full, out_full = fetch_mixer(in_weight, out_weight)
    scale_one = rms_scale(input_complete)
    normalized_rows = (input_complete * scale_one * mixer_f).astype(jnp.bfloat16)
    input_rank_rows = (
        product_simple(normalized_rows, input_adapter_shrink).astype(jnp.bfloat16)
        * adapter_half_float
    )
    projected_rows = jnp.einsum(
        "px,sxa->psa", normalized_rows, in_full, preferred_element_type=jnp.float32
    ) + adapter_scale * jnp.einsum(
        "fw,kwo->fko", input_rank_rows, in_expand, preferred_element_type=jnp.float32
    )
    gate_b = projected_rows[:, 0]
    gate_c = projected_rows[:, 1]
    values_x = projected_rows[:, 2]
    mixed = (gate_b * values_x).astype(jnp.bfloat16)
    prior = shifted(mixed[tok_count - 2 :], "ctx", 1)
    extended = jnp.concatenate([prior, mixed], axis=0).astype(jnp.float32)
    conv_out = (
        conv_w[0] * extended[2:]
        + conv_w[1] * extended[1:-1] * matching_first
        + conv_w[2] * extended[:-2] * matching_second
    )
    gated_rows = (gate_c * conv_out).astype(jnp.bfloat16)
    adapter_branch_sum, output_rank_sum = lax.psum(
        (product_simple(gated_rows, out_full), product_simple(gated_rows, out_shrink)), "tensor"
    )
    output_rank_rows = output_rank_sum.astype(jnp.bfloat16) * adapter_half_float
    hidden_state_rows = input_complete + (
        adapter_branch_sum + adapter_scale * product_simple(output_rank_rows, output_adapter_expand)
    )
    scale_two = rms_scale(hidden_state_rows)
    feedforward_input = (hidden_state_rows * scale_two * ffn_f).astype(jnp.bfloat16)
    feedforward_rank_rows = (
        product_simple(feedforward_input, ffn_shrink).astype(jnp.bfloat16) * pair_bf
    )
    ffn_low_split = feedforward_rank_rows.reshape(tok_count, 2, rank_cols)
    gu_full, down_full = fetch_ffn(gateup_weight, down_weight)
    gate_up_output = jnp.einsum(
        "cm,ame->cae", feedforward_input, gu_full, preferred_element_type=jnp.float32
    ) + adapter_scale * jnp.einsum(
        "vmc,mcb->vmb", ffn_low_split, ffn_expand, preferred_element_type=jnp.float32
    )
    gate_pre = gate_up_output[:, 0]
    up_pre = gate_up_output[:, 1]
    activated_rows = (jax.nn.silu(gate_pre) * up_pre).astype(jnp.bfloat16)
    down_weight_slice = lax.psum_scatter(
        product_simple(activated_rows, down_full).astype(jnp.bfloat16),
        "tensor",
        scatter_dimension=1,
        tiled=True,
    ).astype(jnp.float32)
    down_rank_rows_sum = lax.psum(product_simple(activated_rows, down_shrink), "tensor")
    down_rank_rows = down_rank_rows_sum.astype(jnp.bfloat16) * adapter_half_float
    expand_factor_slice = lax.dynamic_slice_in_dim(
        down_adapter_expand, part_index * half_width, half_width, 1
    )
    hidden_column_slice = lax.dynamic_slice_in_dim(
        hidden_state_rows, part_index * half_width, half_width, 1
    )
    packed_output = (
        hidden_column_slice
        + (down_weight_slice + adapter_scale * product_simple(down_rank_rows, expand_factor_slice))
    ).astype(jnp.bfloat16)
    gu_full, down_full = fetch_ffn(gateup_weight, down_weight)
    down_rank_gradient = (
        adapter_scale * product_backward(cotangent_half_float, down_adapter_expand) * adapter_mask
    ).astype(jnp.bfloat16)
    down_adapter_expand_gradient = adapter_scale * product_leading(
        down_rank_rows, cotangent_half_float
    )
    grad_act = product_backward(cotangent_half_float, down_full) + product_backward(
        down_rank_gradient, down_shrink
    )
    down_shrink_grad = product_leading(activated_rows, down_rank_gradient)
    sigmoid_gate = jax.nn.sigmoid(gate_pre)
    grad_gate = grad_act * up_pre * sigmoid_gate * (1.0 + gate_pre * (1.0 - sigmoid_gate))
    grad_up = grad_act * gate_pre * sigmoid_gate
    grad_gu = jnp.stack([grad_gate, grad_up], axis=1).astype(jnp.bfloat16)
    feedforward_expand_gradient = adapter_scale * jnp.einsum(
        "tje,tjf->jef", ffn_low_split, grad_gu, preferred_element_type=jnp.float32
    )
    feedforward_rank_part = adapter_scale * jnp.einsum(
        "tjf,jef->tje", grad_gu, ffn_expand, preferred_element_type=jnp.float32
    ).reshape(tok_count, 2 * rank_cols)
    ffn_in_part = jnp.einsum("tjf,jdf->td", grad_gu, gu_full, preferred_element_type=jnp.float32)
    ffn_in_sum, ffn_low_sum = lax.psum((ffn_in_part, feedforward_rank_part), "tensor")
    grad_ffn_low = (ffn_low_sum * adapter_mask_pair).astype(jnp.bfloat16)
    grad_ffn_in = ffn_in_sum + product_backward(grad_ffn_low, ffn_shrink)
    ffn_shrink_grad = product_leading(feedforward_input, grad_ffn_low)
    grad_hidden = cot_full + norm_back(hidden_state_rows, scale_two, ffn_f, grad_ffn_in)
    in_full, out_full = fetch_mixer(in_weight, out_weight)
    adapter_branch_gradient = grad_hidden.astype(jnp.bfloat16)
    out_rank_gradient = (
        adapter_scale
        * product_backward(adapter_branch_gradient, output_adapter_expand)
        * adapter_mask
    ).astype(jnp.bfloat16)
    output_expand_gradient = adapter_scale * product_leading(
        output_rank_rows, adapter_branch_gradient
    )
    grad_gated = product_backward(adapter_branch_gradient, out_full) + product_backward(
        out_rank_gradient, out_shrink
    )
    out_shrink_grad = product_leading(gated_rows, out_rank_gradient)
    grad_gate_c = grad_gated * conv_out
    grad_conv = grad_gated * gate_c
    ahead = shifted(grad_conv[:2], "ctx", -1)
    trailing = jnp.concatenate([grad_conv, ahead], axis=0)
    grad_mixed = (
        conv_w[0] * grad_conv
        + conv_w[1] * trailing[1:-1] * ahead_one
        + conv_w[2] * trailing[2:] * ahead_two
    )
    grad_proj = jnp.stack([grad_mixed * values_x, grad_gate_c, grad_mixed * gate_b], axis=1).astype(
        jnp.bfloat16
    )
    input_expand_gradient = adapter_scale * jnp.einsum(
        "te,tjc->jec", input_rank_rows, grad_proj, preferred_element_type=jnp.float32
    )
    input_rank_part = adapter_scale * jnp.einsum(
        "tjc,jec->te", grad_proj, in_expand, preferred_element_type=jnp.float32
    )
    normed_part = jnp.einsum("tjc,jdc->td", grad_proj, in_full, preferred_element_type=jnp.float32)
    normed_sum, input_rank_sum = lax.psum((normed_part, input_rank_part), "tensor")
    in_rank_gradient = (input_rank_sum * adapter_mask).astype(jnp.bfloat16)
    grad_normed = normed_sum + product_backward(in_rank_gradient, input_adapter_shrink)
    in_shrink_grad = product_leading(normalized_rows, in_rank_gradient)
    grad_input_full = grad_hidden + norm_back(input_complete, scale_one, mixer_f, grad_normed)
    packed_grad = lax.dynamic_slice_in_dim(grad_input_full, part_index * half_width, half_width, 1)
    output_blocks = jnp.take(
        packed_output.reshape(group_total, block_rows, half_width), inverse_row, axis=0
    )
    grad_blocks = jnp.take(
        packed_grad.reshape(group_total, block_rows, half_width), inverse_row, axis=0
    )
    block_output = lax.all_to_all(
        output_blocks, "dp", split_axis=0, concat_axis=0, tiled=True
    ).reshape(tok_count, half_width)
    input_grad = (
        lax.all_to_all(
            grad_blocks.astype(jnp.bfloat16), "dp", split_axis=0, concat_axis=0, tiled=True
        )
        .astype(grad_blocks.dtype)
        .reshape(tok_count, half_width)
    )
    totals = lax.psum(
        (
            in_shrink_grad,
            input_expand_gradient,
            out_shrink_grad,
            output_expand_gradient,
            ffn_shrink_grad,
            feedforward_expand_gradient,
            down_shrink_grad,
            down_adapter_expand_gradient,
        ),
        ("dp", "ctx"),
    )
    return (
        block_output,
        input_grad,
        totals[0],
        totals[1],
        totals[2],
        totals[3],
        totals[4],
        totals[5],
        totals[6],
        totals[7],
    )


def solution(mesh):
    placed = (
        P(("dp", "ctx"), "tensor"),
        P(("dp", "ctx"), "tensor"),
        P("dp", None),
        P("dp"),
        P("dp"),
        P(),
        P(),
        P(None, "tensor"),
        P(None, "dp", "tensor"),
        P("tensor", "dp"),
        P(None, "dp", "tensor"),
        P("tensor", "dp"),
        P(),
        P(None, None, "tensor"),
        P("tensor", None),
        P(),
        P(),
        P(None, None, "tensor"),
        P("tensor", None),
        P(),
    )
    return jax.shard_map(
        body,
        mesh=mesh,
        in_specs=placed,
        out_specs=(
            P(("dp", "ctx"), "tensor"),
            P(("dp", "ctx"), "tensor"),
            P(),
            P(None, None, "tensor"),
            P("tensor", None),
            P(),
            P(),
            P(None, None, "tensor"),
            P("tensor", None),
            P(),
        ),
        check_vma=False,
    )
```

profile of v0, /device:TPU:0, one launch (start us, length us, event | category | flops | bytes accessed | tf_op | source)
XLA Modules:
  0.0 1380.1 jit_solution(14482190222094816660)
XLA Ops:
  7.2 25.2 %all_to_all.20 = bf16[4,192,1024]{2,1,0:T(8,128)(2,1)} all-to-all(bf16[4,192,1024]{2,1,0:T(8,128)(2,1)} %bitcast.155), channel_id=1, replica_groups=mesh['dp'=4,'ctx'=4,'tensor'=2] {'dp'}, dimensions={0} | all-to-all | bytes 3145728 | tf_op jit(solution)/shard_map/all_to_all | solution.py:95
  39.3 16.7 %all-to-all-done.2 = bf16[4,192,1024]{2,1,0:T(8,128)(2,1)S(1)} async-done(((bf16[4,192,1024]{2,1,0:T(8,128)(2,1)}), bf16[4,192,1024]{2,1,0:T(8,128)(2,1)S(1)}, u32[]{:S(2)}, u32[]{:S(2)}) %all-to-all-start.2) | async-done | bytes 1572896 | tf_op jit(solution)/shard_map/all_to_all | solution.py:102
  65.6 42.4 %all-gather.7.cloned.1.call-done = bf16[768,2048]{1,0:T(8,128)(2,1)} async-done(((bf16[768,1024]{1,0:T(8,128)(2,1)}), bf16[768,2048]{1,0:T(8,128)(2,1)}) %all-gather.7.cloned.1.call-update) | async-done | bytes 3145744 | tf_op jit(solution)/shard_map/all_gather | solution.py:133
  111.9 79.8 %all-gather.9.cloned.1.call-done = bf16[3,2048,1024]{2,1,0:T(8,128)(2,1)} async-done(((bf16[3,512,1024]{2,1,0:T(8,128)(2,1)}), bf16[3,2048,1024]{2,1,0:T(8,128)(2,1)}) %all-gather.9.cloned.1.call-update) | async-done | bytes 12582928 | tf_op jit(solution)/shard_map/all_gather | solution.py:49
  191.7 13.6 fusion.17
  215.4 12.4 all-gather.11.cloned.1.call-done
  227.8 7.4 fusion.72
  237.9 36.9 %all-gather.17.cloned.1.call-done = bf16[768,2048]{1,0:T(8,128)(2,1)} async-done(((bf16[768,1024]{1,0:T(8,128)(2,1)}), bf16[768,2048]{1,0:T(8,128)(2,1)}) %all-gather.17.cloned.1.call-update) | async-done | bytes 3145744 | tf_op jit(solution)/shard_map/all_gather | solution.py:134
  278.3 74.0 %all-gather.15.cloned.1.call-done = bf16[2816,2048]{1,0:T(8,128)(2,1)} async-done(((bf16[2816,512]{1,0:T(8,128)(2,1)}), bf16[2816,2048]{1,0:T(8,128)(2,1)}) %all-gather.15.cloned.1.call-update) | async-done | bytes 11534352 | tf_op jit(solution)/shard_map/all_gather | solution.py:57
  352.3 15.8 %fusion.75 = f32[768,2816]{1,0:T(8,128)} fusion(bf16[768,2048]{1,0:T(8,128)(2,1)} %all-gather.17.cloned.1.call-done, bf16[2816,2048]{1,0:T(8,128)(2,1)} %all-gather.15.cloned.1.call-done), kind=kOutput, calls=%fused_computation.166 | convolution fusion | flops 8858370048 | bytes 23330816 | tf_op jit(solution)/shard_map/dot_general | solution.py:32
  369.5 25.5 %all-reduce.17 = bf16[768,128]{1,0:T(8,128)(2,1)S(1)} all-reduce(f32[768,128]{1,0:T(8,128)} %fusion.73), channel_id=1, replica_groups=mesh['dp'=4,'ctx'=4,'tensor'=2] {'tensor'}, use_global_device_ids=true, to_apply=%region_7.9 | all-reduce | flops 98304 | bytes 589824 | tf_op jit(solution)/shard_map/psum | solution.py:166
  395.0 121.3 %all-reduce.10.cloned.1.call-done = f32[768,2048]{1,0:T(8,128)} async-done(((f32[768,2048]{1,0:T(8,128)}), f32[768,2048]{1,0:T(8,128)}) %all-reduce.10.cloned.1.call-update) | async-done | bytes 6291472 | tf_op jit(solution)/shard_map/psum | solution.py:166
  516.3 4.7 multiply_reduce_fusion.2
  528.2 131.7 %all-gather.13.cloned.1.call-done = bf16[2,2048,2816]{2,1,0:T(8,128)(2,1)} async-done(((bf16[2,512,2816]{2,1,0:T(8,128)(2,1)}), bf16[2,2048,2816]{2,1,0:T(8,128)(2,1)}) %all-gather.13.cloned.1.call-update) | async-done | bytes 23068688 | tf_op jit(solution)/shard_map/all_gather | solution.py:56
  659.9 23.8 %fusion.15 = f32[768,2,2816]{2,0,1:T(8,128)S(1)} fusion(bf16[2,2048,2816]{2,1,0:T(8,128)(2,1)} %all-gather.13.cloned.1.call-done, bf16[768,2048]{1,0:T(8,128)(2,1)} %copy-done.11), kind=kOutput, calls=%fused_computation.57 | convolution fusion | flops 17716740096 | bytes 43515904 | tf_op jit(solution)/shard_map/cm,ame->cae/dot_general | solution.py:180
  683.6 9.4 bitcast_add_fusion
  693.0 13.5 fusion.2
  706.6 5.8 fusion.24
  713.6 25.4 %convolution_bitcast_fusion.1 = f32[768,2048]{1,0:T(8,128)} fusion(bf16[2,2048,2816]{2,1,0:T(8,128)(2,1)} %all-gather.13.cloned.1.call-done, bf16[768,1,2816]{2,0,1:T(8,128)(2,1)} %get-tuple-element.53, bf16[768,1,2816]{2,0,1:T(8,128)(2,1)} %copy-done.65), kind=kOutput, calls=%fused_computation.31 | convolution fusion | flops 17721065472 | bytes 38010880 | tf_op jit(solution)/shard_map/tjf,jdf->td/dot_general | solution.py:227
  739.0 14.4 %convolution_convert_fusion = bf16[768,2048]{1,0:T(8,128)(2,1)} fusion(bf16[768,2816]{1,0:T(8,128)(2,1)} %get-tuple-element.54, bf16[2816,2048]{1,0:T(8,128)(2,1)} %all-gather.15.cloned.1.call-done), kind=kOutput, calls=%fused_computation.32 | convolution fusion | flops 8859942912 | bytes 19005440 | tf_op jit(solution)/shard_map/dot_general | solution.py:28
  753.6 156.1 %all-reduce.16.cloned.1.call-done = (f32[768,2048]{1,0:T(8,128)}, f32[768,256]{1,0:T(8,128)}) async-done(((f32[768,2048]{1,0:T(8,128)}, f32[768,256]{1,0:T(8,128)}), (f32[768,2048]{1,0:T(8,128)}, f32[768,256]{1,0:T(8,128)})) %all-reduce.16.cloned.1.call-update) | async-done | bytes 7077904 | tf_op jit(solution)/shard_map/psum | solution.py:228
  909.7 6.5 multiply_reduce_fusion.1
  930.6 4.2 collective-permute-done.1
  940.3 14.7 %convolution_bitcast_fusion = f32[768,2048]{1,0:T(8,128)} fusion(bf16[3,2048,1024]{2,1,0:T(8,128)(2,1)} %all-gather.9.cloned.1.call-done, bf16[768,1,1024]{2,0,1:T(8,128)(2,1)S(1)} %fusion.23, bf16[768,1,1024]{2,0,1:T(8,128)(2,1)S(1)} %get-tuple-element.57, bf16[768,1,1024]{2,0,1:T(8,128)(2,1)S(1)} %get-tuple-element.48), kind=kOutput, calls=%fused_computation.30 | convolution fusion | flops 9668395008 | bytes 23592960 | tf_op jit(solution)/shard_map/tjc,jdc->td/dot_general | solution.py:265
  959.1 4.8 fusion.77
  963.9 6.9 convolution_multiply_fusion
  978.8 41.3 %all-reduce.18 = (bf16[768,128]{1,0:T(8,128)(2,1)S(1)}, bf16[768,128]{1,0:T(8,128)(2,1)S(1)}) all-reduce(f32[768,128]{1,0:T(8,128)S(1)} %fusion.74, f32[768,128]{1,0:T(8,128)S(1)} %fusion.27), channel_id=1, replica_groups=mesh['dp'=4,'ctx'=4,'tensor'=2] {'tensor'}, use_global_device_ids=true, to_apply=%region_10.12 | all-reduce | flops 196608 | bytes 1179648 | tf_op jit(solution)/shard_map/psum | solution.py:194
  1035.0 92.8 %all-reduce.12.cloned.1.call-done = f32[768,2048]{1,0:T(8,128)} async-done(((f32[768,2048]{1,0:T(8,128)}), f32[768,2048]{1,0:T(8,128)}) %all-reduce.12.cloned.1.call-update) | async-done | bytes 6291472 | tf_op jit(solution)/shard_map/psum | solution.py:266
  1127.8 4.9 multiply_reduce_fusion
  1141.1 39.8 %all_to_all.21 = bf16[4,192,1024]{2,1,0:T(8,128)(2,1)S(1)} all-to-all(bf16[4,192,1024]{2,1,0:T(8,128)(2,1)S(1)} %get-tuple-element.67), channel_id=1, replica_groups=mesh['dp'=4,'ctx'=4,'tensor'=2] {'dp'}, dimensions={0} | all-to-all | bytes 3145728 | tf_op jit(solution)/shard_map/all_to_all | solution.py:278
  1180.9 4.4 all-to-all-start.3
  1185.3 170.9 %all-reduce.14.cloned.1.call-done = (f32[2048,128]{1,0:T(8,128)}, f32[3,128,1024]{1,2,0:T(8,128)}, f32[1024,128]{1,0:T(8,128)}, f32[128,2048]{1,0:T(8,128)}, f32...) async-done(((f32[2048,128]{1,0:T(8,128)}, f32[3,128,1024]{1,2,0:T(8,128)}, f32[1024,128]{1,0:T(8,128)}, ...) | async-done | bytes 11665424 | tf_op jit(solution)/shard_map/psum | solution.py:288
  (250 shorter events, 117.4 us)
Async XLA Ops:
  7.2 676.5 %copy-start = (bf16[2,128,2816]{2,1,0:T(8,128)(2,1)S(1)}, bf16[2,128,2816]{2,1,0:T(8,128)(2,1)}, u32[]{:S(2)}) copy-start(bf16[2,128,2816]{2,1,0:T(8,128)(2,1)} %param.39) | copy-start | bytes 4325380
  7.2 28.9 %copy-start.63 = (s32[1,4]{1,0:T(1,128)S(1)}, s32[1,4]{1,0:T(1,128)}, u32[]{:S(2)}) copy-start(s32[1,4]{1,0:T(1,128)} %param.24) | copy-start | bytes 52
  32.4 23.6 %all-to-all-start.2 = ((bf16[4,192,1024]{2,1,0:T(8,128)(2,1)}), bf16[4,192,1024]{2,1,0:T(8,128)(2,1)S(1)}, u32[]{:S(2)}, u32[]{:S(2)}) async-start(bf16[4,192,1024]{2,1,0:T(8,128)(2,1)} %bitcast.156), calls=%async_computation.3 | async-start | bytes 3145728 | tf_op jit(solution)/shard_map/all_to_all | solution.py:102
  36.0 72.0 %all-gather.7.cloned.1.call-start = ((), (), s32[]{:S(2)}) async-start(), calls=%async_computation.5 | async-start | bytes 4718592 | tf_op jit(solution)/shard_map/all_gather | solution.py:133
  61.8 130.0 %all-gather.9.cloned.1.call-start = ((), (), s32[]{:S(2)}) async-start(), calls=%async_computation.6 | async-start | bytes 15728640 | tf_op jit(solution)/shard_map/all_gather | solution.py:49
  62.6 165.3 %all-gather.11.cloned.1.call-start = ((), (), s32[]{:S(2)}) async-start(), calls=%async_computation.7 | async-start | bytes 5242880 | tf_op jit(solution)/shard_map/all_gather | solution.py:50
  63.3 211.5 %all-gather.17.cloned.1.call-start = ((), (), s32[]{:S(2)}) async-start(), calls=%async_computation.12 | async-start | bytes 4718592 | tf_op jit(solution)/shard_map/all_gather | solution.py:134
  63.9 46.9 %copy-start.38 = (bf16[2048,128]{1,0:T(8,128)(2,1)S(1)}, bf16[2048,128]{1,0:T(8,128)(2,1)}, u32[]{:S(2)}) copy-start(bf16[2048,128]{1,0:T(8,128)(2,1)} %param.34) | copy-start | bytes 1572868
  63.9 288.5 %all-gather.15.cloned.1.call-start = ((), (), s32[]{:S(2)}) async-start(), calls=%async_computation.10 | async-start | bytes 14417920 | tf_op jit(solution)/shard_map/all_gather | solution.py:57
  64.5 451.9 %all-reduce.10.cloned.1.call-start = ((), (), s32[]{:S(2)}) async-start(), calls=%async_computation.8 | async-start | bytes 12582912 | tf_op jit(solution)/shard_map/psum | solution.py:166
  64.5 127.2 %copy-start.54 = (f32[2048]{0:T(1024)}, f32[2048]{0:T(1024)S(1)}, u32[]{:S(2)}) copy-start(f32[2048]{0:T(1024)S(1)} %convert_element_type.128) | copy-start | bytes 24580
  110.9 80.9 %copy-start.46 = (f32[768]{0:T(1024)}, f32[768]{0:T(1024)S(1)}, u32[]{:S(2)}) copy-start(f32[768]{0:T(1024)S(1)} %add_rsqrt_fusion.1) | copy-start | bytes 9220
  111.9 93.4 %copy-start.41 = (bf16[768,128,1]{1,0,2:T(8,128)(2,1)}, bf16[768,128,1]{1,0,2:T(8,128)(2,1)S(1)}, u32[]{:S(2)}) copy-start(bf16[768,128,1]{1,0,2:T(8,128)(2,1)S(1)} %fusion.32) | copy-start | bytes 589828
  111.9 93.4 %copy-start.28 = (bf16[3,128,1024]{2,1,0:T(8,128)(2,1)S(1)}, bf16[3,128,1024]{2,1,0:T(8,128)(2,1)}, u32[]{:S(2)}) copy-start(bf16[3,128,1024]{2,1,0:T(8,128)(2,1)} %param.35) | copy-start | bytes 2359300
  207.3 4.7 collective-permute-start
  215.4 152.8 %copy-start.7 = (bf16[768,1024]{1,0:T(8,128)(2,1)}, bf16[768,1024]{1,0:T(8,128)(2,1)S(1)}, u32[]{:S(2)}) copy-start(bf16[768,1024]{1,0:T(8,128)(2,1)S(1)} %get-tuple-element.50) | copy-start | bytes 4718596
  235.2 39.5 %copy-start.44 = (bf16[128,2048]{1,0:T(8,128)(2,1)S(1)}, bf16[128,2048]{1,0:T(8,128)(2,1)}, u32[]{:S(2)}) copy-start(bf16[128,2048]{1,0:T(8,128)(2,1)} %param.41) | copy-start | bytes 1572868
  235.2 424.6 %all-gather.13.cloned.1.call-start = ((), (), s32[]{:S(2)}) async-start(), calls=%async_computation.9 | async-start | bytes 28835840 | tf_op jit(solution)/shard_map/all_gather | solution.py:56
  236.0 673.7 %all-reduce.16.cloned.1.call-start = ((), (), s32[]{:S(2)}) async-start(), calls=%async_computation.15 | async-start | bytes 14155776 | tf_op jit(solution)/shard_map/psum | solution.py:228
  352.3 15.8 %copy-start.32 = (bf16[1024,128]{1,0:T(8,128)(2,1)S(1)}, bf16[1024,128]{1,0:T(8,128)(2,1)}, u32[]{:S(2)}) copy-start(bf16[1024,128]{1,0:T(8,128)(2,1)} %param.36) | copy-start | bytes 786436
  368.2 148.1 %copy-start.14 = (bf16[128,2048]{1,0:T(8,128)(2,1)S(1)}, bf16[128,2048]{1,0:T(8,128)(2,1)}, u32[]{:S(2)}) copy-start(bf16[128,2048]{1,0:T(8,128)(2,1)} %param.37) | copy-start | bytes 1572868
  395.0 126.0 %copy-start.16 = (bf16[768,128]{1,0:T(8,128)(2,1)}, bf16[768,128]{1,0:T(8,128)(2,1)S(1)}, u32[]{:S(2)}) copy-start(bf16[768,128]{1,0:T(8,128)(2,1)S(1)} %all-reduce.17) | copy-start | bytes 589828
  739.0 290.9 %reduce-scatter.2.cloned.1.call-start = ((), (), s32[]{:S(2)}) async-start(), calls=%async_computation.11 | async-start | bytes 4718592 | tf_op jit(solution)/shard_map/reduce_scatter | solution.py:188
  753.5 156.2 %copy-start.26 = (f32[768,128]{1,0:T(8,128)S(1)}, f32[768,128]{1,0:T(8,128)}, u32[]{:S(2)}) copy-start(f32[768,128]{1,0:T(8,128)} %compare_convert_fusion) | copy-start | bytes 1179652
  753.5 156.2 %copy-start.31 = (bf16[2048,256]{1,0:T(8,128)(2,1)S(1)}, bf16[2048,256]{1,0:T(8,128)(2,1)}, u32[]{:S(2)}) copy-start(bf16[2048,256]{1,0:T(8,128)(2,1)} %param.38) | copy-start | bytes 3145732
  753.5 374.3 %all-reduce.12.cloned.1.call-start = ((), (), s32[]{:S(2)}) async-start(), calls=%async_computation.13 | async-start | bytes 12582912 | tf_op jit(solution)/shard_map/psum | solution.py:266
  929.3 5.5 collective-permute-start.1
  955.0 401.1 %all-reduce.14.cloned.1.call-start = ((), (), s32[]{:S(2)}) async-start(), calls=%async_computation.14 | async-start | bytes 23330816 | tf_op jit(solution)/shard_map/psum | solution.py:288
  978.8 45.0 %copy-start.47 = (f32[768]{0:T(1024)S(1)}, f32[768]{0:T(1024)}, u32[]{:S(2)}) copy-start(f32[768]{0:T(1024)} %copy-done.46) | copy-start | bytes 9220
  978.8 45.0 %copy-start.55 = (f32[2048]{0:T(1024)S(1)}, f32[2048]{0:T(1024)}, u32[]{:S(2)}) copy-start(f32[2048]{0:T(1024)} %copy-done.54) | copy-start | bytes 24580
  1033.2 94.6 %copy-start.39 = (bf16[2048,128]{1,0:T(8,128)(2,1)S(1)}, bf16[2048,128]{1,0:T(8,128)(2,1)}, u32[]{:S(2)}) copy-start(bf16[2048,128]{1,0:T(8,128)(2,1)} %param.34) | copy-start | bytes 1572868
  1180.9 178.3 %all-to-all-start.3 = ((bf16[4,192,1024]{2,1,0:T(8,128)(2,1)}), bf16[4,192,1024]{2,1,0:T(8,128)(2,1)}, u32[]{:S(2)}, u32[]{:S(2)}) async-start(bf16[4,192,1024]{2,1,0:T(8,128)(2,1)} %get-tuple-element.66), calls=%async_computation.4 | async-start | bytes 3145728 | tf_op jit(solution)/shard_map/all_to_all | solution.py:282
  (56 other events, 240.8 us)
Sparse Core Ops, SparseCore 0:
  61.9 46.0 all-gather.6
  109.6 82.0 all-gather.8
  193.3 34.4 all-gather.10
  229.8 44.9 all-gather.16
  276.2 76.1 all-gather.14
  354.6 161.6 all-reduce.9
  518.0 141.8 all-gather.12
  739.1 170.5 all-reduce.15
  911.9 43.3 reduce-scatter.1
  957.7 170.0 all-reduce.11
  1133.8 222.3 all-reduce.13
where the time goes:
time: 1390 us; the launch traced here: 1380 us
  waiting for transfers between devices  944 us (68%)
  matrix products  208 us (15%)
  blocking collectives  132 us (9%)
  local copies, waits for them, and re-layouts  36.4 us (3%)
  other arithmetic  31.6 us (2%)
  between operations  15.3 us (1%)
    psum x1, waiting for transfers between devices, body(): lax.psum((in_shrink_grad, input_expand_gradient, out_shrink_grad, output_...  171 us
    psum x1, waiting for transfers between devices, body(): lax.psum((ffn_in_part, feedforward_rank_part), 'tensor')  156 us
    all_gather x1, waiting for transfers between devices, fetch_ffn(): lax.all_gather(gateup_weight, 'dp', axis=1, tiled=True)  132 us
    psum x1, waiting for transfers between devices, body(): lax.psum((product_simple(gated_rows, out_full), product_simple(gated_rows...  121 us
    psum x1, waiting for transfers between devices, body(): lax.psum((normed_part, input_rank_part), 'tensor')  92.8 us
    all_gather x1, waiting for transfers between devices, fetch_mixer(): lax.all_gather(in_weight, 'dp', axis=1, tiled=True)  79.8 us
    all_gather x1, waiting for transfers between devices, fetch_ffn(): lax.all_gather(down_weight, 'dp', axis=1, tiled=True)  74 us
    dot_general x8, matrix products, product_backward(): lax.dot_general(left, right, (((1,), (1,)), ((), ())), preferred_element_...  49.3 us
  transfers between devices with their start and end apart: 15, of which 13 were waited for; matrix products, arithmetic and copies ran while one was open for 12% of the time, Pallas kernels for 0%

commit v1 on v0

--- a/solution.py
+++ b/solution.py
@@ -8,6 +8,26 @@
 adapter_scale = 0.5
 
 
+def step_on_the_sources_all(s0, row_dim):
+    num = lax.psum(1, axis_name="dp")
+    built = range(num)
+    val = map(lambda u: (u, (u + 1) % num), built)
+    block_list = list(val)
+    series = list(map(lambda u: (u, (u - 1) % num), range(num)))
+    top, passed = ([s0], [s0])
+    for _ in range(num // 2):
+        ready = lax.ppermute(top[-1], axis_name="dp", perm=block_list)
+        top.append(ready)
+    j0 = 0
+    while j0 < (num - 1) // 2:
+        upper = lax.ppermute(passed[-1], axis_name="dp", perm=series)
+        passed.append(upper)
+        j0 += 1
+    before = jnp.concatenate([*top[::-1], *passed[1:]], axis=row_dim)
+    z2 = jnp.roll(before, (lax.axis_index("dp") - num // 2) * s0.shape[row_dim], axis=row_dim)
+    return z2
+
+
 def shifted(block, axis, distance):
     devices = range(lax.axis_size(axis))
     route = [(i - distance, i) for i in devices if i - distance in devices]
@@ -54,7 +74,7 @@
 def fetch_ffn(gateup_weight, down_weight):
     return (
         lax.all_gather(gateup_weight, "dp", axis=1, tiled=True),
-        lax.all_gather(down_weight, "dp", axis=1, tiled=True),
+        step_on_the_sources_all(down_weight, 1),
     )
 
 

time: 1390 us -> 1320 us (0.950)
  waiting for transfers between devices: 944 us -> 840 us
  other arithmetic: 31.6 us -> 55.6 us
    ppermute x0 -> x3, waiting for transfers between devices: none -> 87.7 us  [the longest x2 87.7 us: step_on_the_sources_all(): ready = lax.ppermute(top[-1], axis_name='dp', perm=block_list)]
    psum x1, waiting for transfers between devices: 121 us -> 47.1 us  [body(): lax.psum((product_simple(gated_rows, out_full), product_simple(gated_rows...]
    all_gather x1 -> x0, waiting for transfers between devices: 74 us -> none  [fetch_ffn(): lax.all_gather(down_weight, 'dp', axis=1, tiled=True)]
    all_gather x1, waiting for transfers between devices: 36.9 us -> 0.01 us  [body(): lax.all_gather(packed_cot, 'tensor', axis=1, tiled=True)]
    concatenate x0 -> x1, other arithmetic: none -> 19.6 us  [step_on_the_sources_all(): jnp.roll(before, (lax.axis_index('dp') - num // 2) * s0.shape[row_dim], a...]
  transfers between devices with their start and end apart: 15 -> 17, of which waited for: 13 -> 13; matrix products, arithmetic and copies ran while one was open for 12% -> 14% of each run, Pallas kernels for 0% -> 0%
where the time goes in v1:
time: 1320 us; the launch traced here: 1310 us
  waiting for transfers between devices  840 us (64%)
  matrix products  205 us (16%)
  blocking collectives  130 us (10%)
  other arithmetic  55.6 us (4%)
  local copies, waits for them, and re-layouts  36.4 us (3%)
  starting transfers between devices  27.1 us (2%)
  between operations  15.4 us (1%)
    psum x1, waiting for transfers between devices, body(): lax.psum((in_shrink_grad, input_expand_gradient, out_shrink_grad, output_...  171 us
    psum x1, waiting for transfers between devices, body(): lax.psum((ffn_in_part, feedforward_rank_part), 'tensor')  156 us
    all_gather x1, waiting for transfers between devices, fetch_ffn(): lax.all_gather(gateup_weight, 'dp', axis=1, tiled=True)  132 us
    psum x1, waiting for transfers between devices, body(): lax.psum((normed_part, input_rank_part), 'tensor')  88.4 us
    ppermute x2, waiting for transfers between devices, step_on_the_sources_all(): ready = lax.ppermute(top[-1], axis_name='dp', perm=block_list)  87.7 us
    all_gather x1, waiting for transfers between devices, fetch_mixer(): lax.all_gather(in_weight, 'dp', axis=1, tiled=True)  78.1 us
    psum x1, waiting for transfers between devices, body(): lax.psum((product_simple(gated_rows, out_full), product_simple(gated_rows...  47.1 us
    dot_general x8, matrix products, product_backward(): lax.dot_general(left, right, (((1,), (1,)), ((), ())), preferred_element_...  46.9 us
  transfers between devices with their start and end apart: 17, of which 13 were waited for; matrix products, arithmetic and copies ran while one was open for 14% of the time, Pallas kernels for 0%

profile of v1, /device:TPU:0, one launch (start us, length us, event | category | flops | bytes accessed | tf_op | source)
XLA Modules:
  0.0 1309.4 jit_solution(7512923251683657324)
XLA Ops:
  7.2 25.2 %all_to_all.20 = bf16[4,192,1024]{2,1,0:T(8,128)(2,1)} all-to-all(bf16[4,192,1024]{2,1,0:T(8,128)(2,1)} %bitcast.155), channel_id=1, replica_groups=mesh['dp'=4,'ctx'=4,'tensor'=2] {'dp'}, dimensions={0} | all-to-all | bytes 3145728 | tf_op jit(solution)/shard_map/all_to_all | solution.py:115
  39.3 16.8 %all-to-all-done.2 = bf16[4,192,1024]{2,1,0:T(8,128)(2,1)S(1)} async-done(((bf16[4,192,1024]{2,1,0:T(8,128)(2,1)}), bf16[4,192,1024]{2,1,0:T(8,128)(2,1)S(1)}, u32[]{:S(2)}, u32[]{:S(2)}) %all-to-all-start.2) | async-done | bytes 1572896 | tf_op jit(solution)/shard_map/all_to_all | solution.py:122
  64.5 43.5 %all-gather.6.cloned.1.call-done = bf16[768,2048]{1,0:T(8,128)(2,1)} async-done(((bf16[768,1024]{1,0:T(8,128)(2,1)}), bf16[768,2048]{1,0:T(8,128)(2,1)}) %all-gather.6.cloned.1.call-update) | async-done | bytes 3145744 | tf_op jit(solution)/shard_map/all_gather | solution.py:153
  113.6 78.1 %all-gather.8.cloned.1.call-done = bf16[3,2048,1024]{2,1,0:T(8,128)(2,1)} async-done(((bf16[3,512,1024]{2,1,0:T(8,128)(2,1)}), bf16[3,2048,1024]{2,1,0:T(8,128)(2,1)}) %all-gather.8.cloned.1.call-update) | async-done | bytes 12582928 | tf_op jit(solution)/shard_map/all_gather | solution.py:69
  191.7 13.6 %fusion.24 = f32[768,3,1024]{2,0,1:T(8,128)S(1)} fusion(bf16[3,2048,1024]{2,1,0:T(8,128)(2,1)} %all-gather.8.cloned.1.call-done, f32[2048]{0:T(1024)S(1)} %convert_element_type.128, f32[768]{0:T(1024)S(1)} %add_rsqrt_fusion.1, bf16[768,2048]{1,0:T(8,128)(2,1)} %all-gather.6.cloned.1.call-done), kind=kOutput, calls=%fused_computation.74 | convolution fusion | flops 9669967872 | bytes 25177088 | tf_op jit(solution)/shard_map/px,sxa->psa/dot_general | solution.py:169
  215.4 12.4 all-gather.10.cloned.1.call-done
  227.8 7.4 fusion.80
  237.7 62.8 %collective-permute-done.1 = bf16[2816,512]{1,0:T(8,128)(2,1)} collective-permute-done((bf16[2816,512]{1,0:T(8,128)(2,1)}, bf16[2816,512]{1,0:T(8,128)(2,1)}, u32[]{:S(2)}, u32[]{:S(2)}) %collective-permute-start.1) | collective-permute-done | bytes 2883616 | tf_op jit(solution)/shard_map/ppermute | solution.py:19
  300.5 12.1 collective-permute-start.2
  317.2 4.7 fusion.83
  321.9 24.9 %collective-permute-done.2 = bf16[2816,512]{1,0:T(8,128)(2,1)} collective-permute-done((bf16[2816,512]{1,0:T(8,128)(2,1)}, bf16[2816,512]{1,0:T(8,128)(2,1)}, u32[]{:S(2)}, u32[]{:S(2)}) %collective-permute-start.2) | collective-permute-done | bytes 2883616 | tf_op jit(solution)/shard_map/ppermute | solution.py:19
  346.8 19.6 %fusion.3 = bf16[2816,2048]{1,0:T(8,128)(2,1)} fusion(s32[]{:T(128)S(6)} %select_n.72, bf16[2816,512]{1,0:T(8,128)(2,1)} %collective-permute-done.2, bf16[2816,512]{1,0:T(8,128)(2,1)} %collective-permute-done.1, bf16[2816,512]{1,0:T(8,128)(2,1)S(1)} %copy-done.12, bf16[2816,512]{1,0:T(8,128)(2,1)} %collective-permute-done.3), kind=kLoop, calls=%fused_computation.16 | loop fusion | flops 92274688 | bytes 23068676 | tf_op jit(solution)/shard_map/jit(_roll_dynamic)/concatenate | solution.py:27
  367.7 23.9 %all-reduce.17 = bf16[768,128]{1,0:T(8,128)(2,1)S(1)} all-reduce(f32[768,128]{1,0:T(8,128)} %fusion.81), channel_id=1, replica_groups=mesh['dp'=4,'ctx'=4,'tensor'=2] {'tensor'}, use_global_device_ids=true, to_apply=%region_7.9 | all-reduce | flops 98304 | bytes 589824 | tf_op jit(solution)/shard_map/psum | solution.py:186
  391.6 47.1 %all-reduce.10.cloned.1.call-done = f32[768,2048]{1,0:T(8,128)} async-done(((f32[768,2048]{1,0:T(8,128)}), f32[768,2048]{1,0:T(8,128)}) %all-reduce.10.cloned.1.call-update) | async-done | bytes 6291472 | tf_op jit(solution)/shard_map/psum | solution.py:186
  438.7 4.7 multiply_reduce_fusion.2
  450.0 132.1 %all-gather.12.cloned.1.call-done = bf16[2,2048,2816]{2,1,0:T(8,128)(2,1)} async-done(((bf16[2,512,2816]{2,1,0:T(8,128)(2,1)}), bf16[2,2048,2816]{2,1,0:T(8,128)(2,1)}) %all-gather.12.cloned.1.call-update) | async-done | bytes 23068688 | tf_op jit(solution)/shard_map/all_gather | solution.py:76
  582.1 23.8 %fusion.22 = f32[768,2,2816]{2,0,1:T(8,128)S(1)} fusion(bf16[2,2048,2816]{2,1,0:T(8,128)(2,1)} %all-gather.12.cloned.1.call-done, bf16[768,2048]{1,0:T(8,128)(2,1)} %copy-done.10), kind=kOutput, calls=%fused_computation.72 | convolution fusion | flops 17716740096 | bytes 43515904 | tf_op jit(solution)/shard_map/cm,ame->cae/dot_general | solution.py:200
  605.9 8.4 bitcast_add_fusion
  614.3 22.8 %fusion.9 = (bf16[768,1,2816]{2,0,1:T(8,128)(2,1)}, bf16[768,1,2816]{2,0,1:T(8,128)(2,1)}, bf16[768,2816]{1,0:T(8,128)(2,1)}) fusion(f32[768,2,2816]{2,0,1:T(8,128)} %bitcast_add_fusion, f32[768,2816]{1,0:T(8,128)} %fusion.83, bf16[768,2048]{1,0:T(8,128)(2,1)} %all-gather.14.cloned.1.call-done, bf16[2816,2048]{1,0:T(8,128)(2,1)} %fusion.3), kind=kOutput, calls=%fused_computation.43 | convolution fusion | flops 8895135744 | bytes 53608448 | tf_op jit(solution)/shard_map/dot_general | solution.py:52
  637.1 5.1 fusion.31
  643.3 25.0 %convolution_bitcast_fusion.1 = f32[768,2048]{1,0:T(8,128)} fusion(bf16[2,2048,2816]{2,1,0:T(8,128)(2,1)} %all-gather.12.cloned.1.call-done, bf16[768,1,2816]{2,0,1:T(8,128)(2,1)} %get-tuple-element.54, bf16[768,1,2816]{2,0,1:T(8,128)(2,1)} %get-tuple-element.53), kind=kOutput, calls=%fused_computation.46 | convolution fusion | flops 17721065472 | bytes 38010880 | tf_op jit(solution)/shard_map/tjf,jdf->td/dot_general | solution.py:247
  668.4 14.4 %convolution_convert_fusion = bf16[768,2048]{1,0:T(8,128)(2,1)} fusion(bf16[768,2816]{1,0:T(8,128)(2,1)} %get-tuple-element.55, bf16[2816,2048]{1,0:T(8,128)(2,1)} %fusion.3), kind=kOutput, calls=%fused_computation.47 | convolution fusion | flops 8859942912 | bytes 19005440 | tf_op jit(solution)/shard_map/dot_general | solution.py:48
  682.9 156.2 %all-reduce.16.cloned.1.call-done = (f32[768,2048]{1,0:T(8,128)}, f32[768,256]{1,0:T(8,128)}) async-done(((f32[768,2048]{1,0:T(8,128)}, f32[768,256]{1,0:T(8,128)}), (f32[768,2048]{1,0:T(8,128)}, f32[768,256]{1,0:T(8,128)})) %all-reduce.16.cloned.1.call-update) | async-done | bytes 7077904 | tf_op jit(solution)/shard_map/psum | solution.py:248
  839.1 6.5 multiply_reduce_fusion.1
  870.0 14.8 %convolution_bitcast_fusion = f32[768,2048]{1,0:T(8,128)} fusion(bf16[3,2048,1024]{2,1,0:T(8,128)(2,1)} %all-gather.8.cloned.1.call-done, bf16[768,1,1024]{2,0,1:T(8,128)(2,1)S(1)} %fusion.30, bf16[768,1,1024]{2,0,1:T(8,128)(2,1)S(1)} %get-tuple-element.58, bf16[768,1,1024]{2,0,1:T(8,128)(2,1)S(1)} %get-tuple-element.49), kind=kOutput, calls=%fused_computation.45 | convolution fusion | flops 9668395008 | bytes 23592960 | tf_op jit(solution)/shard_map/tjc,jdc->td/dot_general | solution.py:285
  890.2 4.8 fusion.85
  895.0 6.8 convolution_multiply_fusion
  909.6 40.9 %all-reduce.18 = (bf16[768,128]{1,0:T(8,128)(2,1)S(1)}, bf16[768,128]{1,0:T(8,128)(2,1)S(1)}) all-reduce(f32[768,128]{1,0:T(8,128)S(1)} %copy-done.31, f32[768,128]{1,0:T(8,128)S(1)} %fusion.34), channel_id=1, replica_groups=mesh['dp'=4,'ctx'=4,'tensor'=2] {'tensor'}, use_global_device_ids=true, to_apply=%region_10.13 | all-reduce | flops 196608 | bytes 1179648 | tf_op jit(solution)/shard_map/psum | solution.py:214
  969.0 88.4 %all-reduce.12.cloned.1.call-done = f32[768,2048]{1,0:T(8,128)} async-done(((f32[768,2048]{1,0:T(8,128)}), f32[768,2048]{1,0:T(8,128)}) %all-reduce.12.cloned.1.call-update) | async-done | bytes 6291472 | tf_op jit(solution)/shard_map/psum | solution.py:286
  1057.4 4.9 multiply_reduce_fusion
  1070.7 39.8 %all_to_all.21 = bf16[4,192,1024]{2,1,0:T(8,128)(2,1)S(1)} all-to-all(bf16[4,192,1024]{2,1,0:T(8,128)(2,1)S(1)} %get-tuple-element.68), channel_id=1, replica_groups=mesh['dp'=4,'ctx'=4,'tensor'=2] {'dp'}, dimensions={0} | all-to-all | bytes 3145728 | tf_op jit(solution)/shard_map/all_to_all | solution.py:298
  1114.9 170.6 %all-reduce.14.cloned.1.call-done = (f32[2048,128]{1,0:T(8,128)}, f32[3,128,1024]{1,2,0:T(8,128)}, f32[1024,128]{1,0:T(8,128)}, f32[128,2048]{1,0:T(8,128)}, f32...) async-done(((f32[2048,128]{1,0:T(8,128)}, f32[3,128,1024]{1,2,0:T(8,128)}, f32[1024,128]{1,0:T(8,128)}, ...) | async-done | bytes 11665424 | tf_op jit(solution)/shard_map/psum | solution.py:308
  (273 shorter events, 131.9 us)
Async XLA Ops:
  7.2 598.7 %copy-start = (bf16[2,128,2816]{2,1,0:T(8,128)(2,1)S(1)}, bf16[2,128,2816]{2,1,0:T(8,128)(2,1)}, u32[]{:S(2)}) copy-start(bf16[2,128,2816]{2,1,0:T(8,128)(2,1)} %param.41) | copy-start | bytes 4325380
  32.4 23.6 %all-to-all-start.2 = ((bf16[4,192,1024]{2,1,0:T(8,128)(2,1)}), bf16[4,192,1024]{2,1,0:T(8,128)(2,1)S(1)}, u32[]{:S(2)}, u32[]{:S(2)}) async-start(bf16[4,192,1024]{2,1,0:T(8,128)(2,1)} %bitcast.156), calls=%async_computation.3 | async-start | bytes 3145728 | tf_op jit(solution)/shard_map/all_to_all | solution.py:122
  36.0 72.0 %all-gather.6.cloned.1.call-start = ((), (), s32[]{:S(2)}) async-start(), calls=%async_computation.5 | async-start | bytes 4718592 | tf_op jit(solution)/shard_map/all_gather | solution.py:153
  61.8 129.9 %all-gather.8.cloned.1.call-start = ((), (), s32[]{:S(2)}) async-start(), calls=%async_computation.6 | async-start | bytes 15728640 | tf_op jit(solution)/shard_map/all_gather | solution.py:69
  62.5 165.3 %all-gather.10.cloned.1.call-start = ((), (), s32[]{:S(2)}) async-start(), calls=%async_computation.7 | async-start | bytes 5242880 | tf_op jit(solution)/shard_map/all_gather | solution.py:70
  63.3 250.9 %all-gather.14.cloned.1.call-start = ((), (), s32[]{:S(2)}) async-start(), calls=%async_computation.11 | async-start | bytes 4718592 | tf_op jit(solution)/shard_map/all_gather | solution.py:154
  63.3 128.4 %copy-start.62 = (f32[2048]{0:T(1024)}, f32[2048]{0:T(1024)S(1)}, u32[]{:S(2)}) copy-start(f32[2048]{0:T(1024)S(1)} %convert_element_type.128) | copy-start | bytes 24580
  63.5 375.1 %copy-start.64 = (s32[128]{0:T(128)}, s32[128]{0:T(128)S(1)}, u32[]{:S(2)}) copy-start(s32[128]{0:T(128)S(1)} %and_select_fusion) | copy-start | bytes 1540
  63.8 374.9 %copy-start.48 = (s32[768]{0:T(1024)}, s32[768]{0:T(1024)S(1)}, u32[]{:S(2)}) copy-start(s32[768]{0:T(1024)S(1)} %select_reduce_fusion) | copy-start | bytes 9220
  64.4 374.3 %all-reduce.10.cloned.1.call-start = ((), (), s32[]{:S(2)}) async-start(), calls=%async_computation.8 | async-start | bytes 12582912 | tf_op jit(solution)/shard_map/psum | solution.py:186
  110.6 81.1 %copy-start.54 = (f32[768]{0:T(1024)}, f32[768]{0:T(1024)S(1)}, u32[]{:S(2)}) copy-start(f32[768]{0:T(1024)S(1)} %add_rsqrt_fusion.1) | copy-start | bytes 9220
  113.6 91.8 %copy-start.50 = (bf16[768,128,1]{1,0,2:T(8,128)(2,1)}, bf16[768,128,1]{1,0,2:T(8,128)(2,1)S(1)}, u32[]{:S(2)}) copy-start(bf16[768,128,1]{1,0,2:T(8,128)(2,1)S(1)} %fusion.39) | copy-start | bytes 589828
  113.6 91.8 %copy-start.33 = (bf16[3,128,1024]{2,1,0:T(8,128)(2,1)S(1)}, bf16[3,128,1024]{2,1,0:T(8,128)(2,1)}, u32[]{:S(2)}) copy-start(bf16[3,128,1024]{2,1,0:T(8,128)(2,1)} %param.37) | copy-start | bytes 2359300
  207.3 4.7 collective-permute-start
  215.4 150.9 %copy-start.6 = (bf16[768,1024]{1,0:T(8,128)(2,1)}, bf16[768,1024]{1,0:T(8,128)(2,1)S(1)}, u32[]{:S(2)}) copy-start(bf16[768,1024]{1,0:T(8,128)(2,1)S(1)} %get-tuple-element.51) | copy-start | bytes 4718596
  235.2 79.0 %copy-start.52 = (bf16[128,2048]{1,0:T(8,128)(2,1)S(1)}, bf16[128,2048]{1,0:T(8,128)(2,1)}, u32[]{:S(2)}) copy-start(bf16[128,2048]{1,0:T(8,128)(2,1)} %param.43) | copy-start | bytes 1572868
  235.3 346.9 %all-gather.12.cloned.1.call-start = ((), (), s32[]{:S(2)}) async-start(), calls=%async_computation.9 | async-start | bytes 28835840 | tf_op jit(solution)/shard_map/all_gather | solution.py:76
  235.8 603.3 %all-reduce.16.cloned.1.call-start = ((), (), s32[]{:S(2)}) async-start(), calls=%async_computation.14 | async-start | bytes 14155776 | tf_op jit(solution)/shard_map/psum | solution.py:248
  235.9 64.6 %collective-permute-start.1 = (bf16[2816,512]{1,0:T(8,128)(2,1)}, bf16[2816,512]{1,0:T(8,128)(2,1)}, u32[]{:S(2)}, u32[]{:S(2)}) collective-permute-start(bf16[2816,512]{1,0:T(8,128)(2,1)} %param.35), channel_id=1, source_target_pairs={{0,8},{8,16},{16,24},{24,0},{1,9},{9,17},{17,25},{25,1},{2,10},{10... | collective-permute-start | bytes 8650760 | tf_op jit(solution)/shard_map/ppermute | solution.py:19
  236.2 85.7 %collective-permute-start.3 = (bf16[2816,512]{1,0:T(8,128)(2,1)}, bf16[2816,512]{1,0:T(8,128)(2,1)}, u32[]{:S(2)}, u32[]{:S(2)}) collective-permute-start(bf16[2816,512]{1,0:T(8,128)(2,1)} %param.35), channel_id=1, source_target_pairs={{0,24},{8,0},{16,8},{24,16},{1,25},{9,1},{17,9},{25,17},{2,26},{10... | collective-permute-start | bytes 8650760 | tf_op jit(solution)/shard_map/ppermute | solution.py:23
  300.5 46.3 %collective-permute-start.2 = (bf16[2816,512]{1,0:T(8,128)(2,1)}, bf16[2816,512]{1,0:T(8,128)(2,1)}, u32[]{:S(2)}, u32[]{:S(2)}) collective-permute-start(bf16[2816,512]{1,0:T(8,128)(2,1)} %collective-permute-done.1), channel_id=1, source_target_pairs={{0,8},{8,16},{16,24},{24,0},{1,9},{9,17},{17,25},{25,1},{2,10},{10... | collective-permute-start | bytes 8650760 | tf_op jit(solution)/shard_map/ppermute | solution.py:19
  366.3 72.4 %copy-start.16 = (bf16[128,2048]{1,0:T(8,128)(2,1)S(1)}, bf16[128,2048]{1,0:T(8,128)(2,1)}, u32[]{:S(2)}) copy-start(bf16[128,2048]{1,0:T(8,128)(2,1)} %param.39) | copy-start | bytes 1572868
  391.6 51.8 %copy-start.19 = (bf16[768,128]{1,0:T(8,128)(2,1)}, bf16[768,128]{1,0:T(8,128)(2,1)S(1)}, u32[]{:S(2)}) copy-start(bf16[768,128]{1,0:T(8,128)(2,1)S(1)} %all-reduce.17) | copy-start | bytes 589828
  450.0 155.9 %copy-start.21 = (bf16[768,256]{0,1:T(8,128)(2,1)}, bf16[768,256]{0,1:T(8,128)(2,1)S(1)}, u32[]{:S(2)}) copy-start(bf16[768,256]{0,1:T(8,128)(2,1)S(1)} %copy.45) | copy-start | bytes 1179652
  668.4 294.4 %reduce-scatter.2.cloned.1.call-start = ((), (), s32[]{:S(2)}) async-start(), calls=%async_computation.10 | async-start | bytes 4718592 | tf_op jit(solution)/shard_map/reduce_scatter | solution.py:208
  682.8 156.2 %copy-start.30 = (f32[768,128]{1,0:T(8,128)S(1)}, f32[768,128]{1,0:T(8,128)}, u32[]{:S(2)}) copy-start(f32[768,128]{1,0:T(8,128)} %compare_convert_fusion) | copy-start | bytes 1179652
  682.8 156.2 %copy-start.38 = (bf16[2048,256]{1,0:T(8,128)(2,1)S(1)}, bf16[2048,256]{1,0:T(8,128)(2,1)}, u32[]{:S(2)}) copy-start(bf16[2048,256]{1,0:T(8,128)(2,1)} %param.40) | copy-start | bytes 3145732
  682.9 374.5 %all-reduce.12.cloned.1.call-start = ((), (), s32[]{:S(2)}) async-start(), calls=%async_computation.12 | async-start | bytes 12582912 | tf_op jit(solution)/shard_map/psum | solution.py:286
  859.0 5.5 collective-permute-start.4
  884.8 400.6 %all-reduce.14.cloned.1.call-start = ((), (), s32[]{:S(2)}) async-start(), calls=%async_computation.13 | async-start | bytes 23330816 | tf_op jit(solution)/shard_map/psum | solution.py:308
  967.2 90.2 %copy-start.46 = (bf16[2048,128]{1,0:T(8,128)(2,1)S(1)}, bf16[2048,128]{1,0:T(8,128)(2,1)}, u32[]{:S(2)}) copy-start(bf16[2048,128]{1,0:T(8,128)(2,1)} %param.36) | copy-start | bytes 1572868
  1110.5 178.0 %all-to-all-start.3 = ((bf16[4,192,1024]{2,1,0:T(8,128)(2,1)}), bf16[4,192,1024]{2,1,0:T(8,128)(2,1)}, u32[]{:S(2)}, u32[]{:S(2)}) async-start(bf16[4,192,1024]{2,1,0:T(8,128)(2,1)} %get-tuple-element.67), calls=%async_computation.4 | async-start | bytes 3145728 | tf_op jit(solution)/shard_map/all_to_all | solution.py:302
  (67 other events, 487.8 us)
Sparse Core Ops, SparseCore 0:
  61.9 46.0 all-gather.5
  109.6 82.0 all-gather.7
  193.3 34.4 all-gather.9
  229.8 44.9 all-gather.13
  277.0 161.6 all-reduce.9
  440.2 141.8 all-gather.11
  668.5 170.5 all-reduce.15
  841.3 43.3 reduce-scatter.1
  887.3 170.0 all-reduce.11
  1063.2 222.1 all-reduce.13
